TPU v7x, 512 devices: a whole 4x8x8 slice. The times are simulated.
512 devices in a mesh: vocab: 4 (over x), rows: 128 (over y, z, core).
Axes of the slice: x: 4, y: 8, z: 8, core: 2. Of those that a mesh axis runs over, the one named last changes fastest.
Arguments:
- hidden: bfloat16 [4, 4096, 8192], P(None, 'rows'), may hold values from -0.75 to 0.75
- teacher_weight: bfloat16 [8192, 1536], P('rows', 'vocab'), may hold values from -20 to 20
- draft_weight: bfloat16 [8192, 512], P('rows', 'vocab'), may hold values from -20 to 20
- draft_list: int32 [4, 4], replicated, may hold values from 0 to 11, as said below
Outputs:
- row_loss: float32 [4, 4096], P(None, 'rows')
- grad_hidden: bfloat16 [4, 4096, 8192], P(None, 'rows')
- grad_draft: float32 [8192, 512], P('rows', 'vocab')
Inputs may be any that keep to these rules, and one draw needn't show every extreme that they name: `draft_list`: in each tile the 4 listed blocks are distinct.
All inputs are finite; a program needn't handle non-finite values.
Results may differ from a plain program's by a relative error of at most 0.008.
Values may be sent and summed in bfloat16 or wider, within the bound.
A program may use at most 64 MiB of HBM per device.

v0:
```python
import jax
import jax.numpy as jnp
from jax import lax
from jax.sharding import PartitionSpec as P

BLK = 128


def pick_blocks(tile_blocks, listed):
    return jnp.take(tile_blocks, listed, axis=1)


def per_device(hidden, teacher_weight, draft_weight, draft_list):
    tile_count, tile_rows, model_width = hidden.shape
    row_count = tile_count * tile_rows
    flat_rows = hidden.reshape(row_count, model_width)
    draft_cols = draft_weight.shape[1]
    slot_count = draft_cols // BLK
    columns = flat_rows
    teacher_logits = jnp.dot(
        columns,
        lax.all_gather(teacher_weight, "rows", axis=0, tiled=True),
        preferred_element_type=jnp.float32,
    )
    draft_full = lax.all_gather(draft_weight, "rows", axis=0, tiled=True)
    draft_logits = jnp.dot(flat_rows, draft_full, preferred_element_type=jnp.float32)
    teacher_all = lax.all_gather(teacher_logits, "vocab", axis=1, tiled=True)
    teacher_max = jnp.max(teacher_all, axis=1, keepdims=True)
    teacher_total = jnp.sum(jnp.exp(teacher_all - teacher_max), axis=1, keepdims=True)
    blocks = teacher_all.reshape(tile_count, tile_rows, -1, BLK)
    picked = jax.vmap(pick_blocks)(blocks, draft_list)
    target = jnp.exp(
        picked - teacher_max.reshape(tile_count, tile_rows, 1, 1)
    ) / teacher_total.reshape(tile_count, tile_rows, 1, 1)
    covered = jnp.sum(target, axis=(2, 3)).reshape(row_count)
    vocab_position = lax.axis_index("vocab")
    own_target = lax.dynamic_slice_in_dim(
        target, vocab_position * slot_count, slot_count, 2
    ).reshape(row_count, draft_cols)
    local_max = jnp.max(draft_logits, axis=1)
    weighted = jnp.sum(own_target * draft_logits, axis=1)
    draft_max = lax.pmax(local_max, "vocab")
    local_total = jnp.sum(jnp.exp(draft_logits - draft_max[:, None]), axis=1)
    draft_total, crossed = lax.psum((local_total, weighted), "vocab")
    row_loss = covered * (draft_max + jnp.log(draft_total)) - crossed
    draft_prob = jnp.exp(draft_logits - draft_max[:, None]) / draft_total[:, None]
    logit_grad = (covered[:, None] * draft_prob - own_target).astype(jnp.bfloat16)
    partial_value = lax.dot_general(
        logit_grad, draft_full, (((1,), (1,)), ((), ())), preferred_element_type=jnp.float32
    )
    grad_hidden = lax.psum(partial_value.astype(jnp.bfloat16), "vocab").reshape(
        tile_count, tile_rows, model_width
    )
    columns = flat_rows
    grad_draft = lax.psum_scatter(
        lax.dot_general(
            columns, logit_grad, (((0,), (0,)), ((), ())), preferred_element_type=jnp.float32
        ),
        "rows",
        scatter_dimension=0,
        tiled=True,
    )
    return (row_loss.reshape(tile_count, tile_rows), grad_hidden, grad_draft)


def solution(mesh):
    in_specs = (P(None, "rows", None), P("rows", "vocab"), P("rows", "vocab"), P())
    out_specs = (P(None, "rows"), P(None, "rows", None), P("rows", "vocab"))
    return jax.shard_map(
        per_device, mesh=mesh, in_specs=in_specs, out_specs=out_specs, check_vma=False
    )
```

profile of v0, /device:TPU:1, one launch (start us, length us, event | category | flops | bytes accessed | tf_op | source)
XLA Modules:
  0.0 498.1 jit_solution(2816774992845677760)
XLA Ops:
  7.2 0.0 copy-start
  7.2 0.0 all-gather.5.cloned.1.call-start
  7.2 0.7 all-gather.5.cloned.1.call-update
  7.9 0.0 all-gather.3.cloned.1.call-start
  8.0 0.7 all-gather.3.cloned.1.call-update
  8.7 0.0 all-reduce.3.cloned.1.call-start
  8.7 0.7 compare_and_fusion
  9.4 0.1 copy.16
  9.5 0.7 bitcast_or_fusion
  10.2 0.1 reshape.41
  10.3 89.8 %all-gather.5.cloned.1.call-done = bf16[8192,128]{1,0:T(8,128)(2,1)} async-done(((bf16[64,128]{1,0:T(8,128)(2,1)}), bf16[8192,128]{1,0:T(8,128)(2,1)}) %all-gather.5.cloned.1.call-update) | async-done | bytes 2097168 | tf_op jit(solution)/shard_map/all_gather | solution.py:25
  100.1 0.0 copy-done
  100.1 2.5 fusion.6
  102.6 8.4 %pmax.7 = f32[128]{0:T(128)S(1)} all-reduce(f32[128]{0:T(128)S(1)} %get-tuple-element.18), channel_id=1, replica_groups=mesh['vocab'=4,'rows'=128] {'vocab'}, use_global_device_ids=true, to_apply=%region_4.5 | all-reduce | flops 128 | bytes 1024 | tf_op jit(solution)/shard_map/pmax | solution.py:42
  111.0 75.0 %all-gather.3.cloned.1.call-done = bf16[8192,384]{1,0:T(8,128)(2,1)} async-done(((bf16[64,384]{1,0:T(8,128)(2,1)}), bf16[8192,384]{1,0:T(8,128)(2,1)}) %all-gather.3.cloned.1.call-update) | async-done | bytes 6291472 | tf_op jit(solution)/shard_map/all_gather | solution.py:22
  186.0 4.0 fusion.7
  190.1 11.9 %all_gather.10 = f32[128,1536]{1,0:T(8,128)S(1)} all-gather(f32[128,384]{1,0:T(8,128)S(1)} %fusion.7), channel_id=1, replica_groups=mesh['vocab'=4,'rows'=128] {'vocab'}, dimensions={1}, use_global_device_ids=true | all-gather | bytes 983040 | tf_op jit(solution)/shard_map/all_gather | solution.py:27
  202.0 0.1 reduce_max.18
  202.1 0.3 exponential_reduce_fusion
  202.4 0.1 sub.36
  202.5 1.1 reshape.36
  203.6 0.1 div.18
  203.7 1.5 copy.17
  205.1 0.6 gather_fusion
  205.7 0.2 fusion.4
  206.0 0.1 reshape.37
  206.1 0.1 copy.19
  206.2 7.5 %all-reduce = (f32[128]{0:T(128)S(1)}, f32[128]{0:T(128)S(1)}) all-reduce(f32[128]{0:T(128)S(1)} %get-tuple-element.13, f32[128]{0:T(128)S(1)} %get-tuple-element.12), channel_id=1, replica_groups=mesh['vocab'=4,'rows'=128] {'vocab'}, use_global_device_ids=true, to_apply=%region_8.9 | all-reduce | flops 256 | bytes 2048 | tf_op jit(solution)/shard_map/psum | solution.py:44
  213.8 3.6 convolution_convert_fusion
  217.4 0.0 all-reduce.3.cloned.1.call-update
  217.4 0.0 reduce-scatter.4.cloned.1.call-start
  217.5 2.6 convolution_bitcast_fusion
  220.1 5.6 %copy.22 = f32[8192,128]{1,0:T(8,128)} copy(f32[8192,128]{0,1:T(8,128)} %convolution_bitcast_fusion) | data formatting | bytes 8388608
  225.7 0.0 reduce-scatter.4.cloned.1.call-update
  225.7 0.7 reshape.39
  226.4 59.9 %all-reduce.3.cloned.1.call-done = bf16[4,32,8192]{2,1,0:T(8,128)(2,1)} async-done(((bf16[4,32,8192]{2,1,0:T(8,128)(2,1)}), bf16[4,32,8192]{2,1,0:T(8,128)(2,1)}) %all-reduce.3.cloned.1.call-update) | async-done | bytes 2097168 | tf_op jit(solution)/shard_map/psum | solution.py:51
  286.3 202.1 %reduce-scatter.4.cloned.1.call-done = f32[64,128]{1,0:T(8,128)} async-done(((f32[8192,128]{1,0:T(8,128)}), f32[64,128]{1,0:T(8,128)}) %reduce-scatter.4.cloned.1.call-update) | async-done | bytes 32784
  488.5 3.1 copy.33
  (4 shorter events, 0.1 us)
Async XLA Ops:
  7.2 92.9 %copy-start = (bf16[4,32,8192]{2,1,0:T(8,128)(2,1)S(1)}, bf16[4,32,8192]{2,1,0:T(8,128)(2,1)}, u32[]{:S(2)}) copy-start(bf16[4,32,8192]{2,1,0:T(8,128)(2,1)} %param.4) | copy-start | bytes 6291460
  7.2 92.9 %all-gather.5.cloned.1.call-start = ((), (), s32[]{:S(2)}) async-start(), calls=%async_computation.2 | async-start | bytes 2113536 | tf_op jit(solution)/shard_map/all_gather | solution.py:25
  7.9 178.1 %all-gather.3.cloned.1.call-start = ((), (), s32[]{:S(2)}) async-start(), calls=%async_computation.1 | async-start | bytes 6340608 | tf_op jit(solution)/shard_map/all_gather | solution.py:22
  8.7 277.7 %all-reduce.3.cloned.1.call-start = ((), (), s32[]{:S(2)}) async-start(), calls=%async_computation.3 | async-start | bytes 4194304 | tf_op jit(solution)/shard_map/psum | solution.py:51
  217.4 271.0 %reduce-scatter.4.cloned.1.call-start = ((), (), s32[]{:S(2)}) async-start(), calls=%async_computation.4 | async-start | bytes 4227072
Sparse Core Ops, SparseCore 0:
  11.1 88.9 all-gather.4
  103.2 82.7 all-gather.2
  217.5 68.7 all-reduce.2
  291.1 197.2 reduce-scatter.3
where the time goes:
time: 502 us; the launch traced here: 498 us
  waiting for transfers between devices  428 us (85%)
  blocking collectives  27.8 us (6%)
  between operations  13.8 us (3%)
  local copies, waits for them, and re-layouts  13.1 us (3%)
  matrix products  12.8 us (3%)
    unnamed x5, waiting for transfers between devices  204 us
    all_gather x1, waiting for transfers between devices, per_device(): draft_full = lax.all_gather(draft_weight, 'rows', axis=0, tiled=True)  89.8 us
    all_gather x1, waiting for transfers between devices, per_device(): lax.all_gather(teacher_weight, 'rows', axis=0, tiled=True)  75 us
    psum x1, waiting for transfers between devices, per_device(): lax.psum(partial_value.astype(jnp.bfloat16), 'vocab')  59.9 us
    all_gather x1, blocking collectives, per_device(): teacher_all = lax.all_gather(teacher_logits, 'vocab', axis=1, tiled=True)  11.9 us
  transfers between devices with their start and end apart: 4, of which 4 were waited for; matrix products, arithmetic and copies ran while one was open for 3% of the time, Pallas kernels for 0%

commit v1 on v0

v1 whole, which is shorter than its diff:
```python
import functools
import heapq

import jax
import jax.numpy as jnp
from jax import lax
from jax.experimental import pallas as pl
from jax.experimental.pallas import tpu as pltpu
from jax.sharding import PartitionSpec as P

BLK = 128
F32 = jnp.float32
BF16 = jnp.bfloat16
MESH = pl.DeviceIdType.MESH
NT = (((1,), (1,)), ((), ()))


def offset_of(k):
    return 0 if k == 0 else (-(k + 1) // 2 if k % 2 else k // 2)


def reach(ring, kind, k):
    half = ring // 2
    if kind == "P" or k % 2 == 0:
        return {"R": half, "L": half - 1}
    return {"R": half - 1, "L": half}


def follow(ring, event):
    kind, k, way, dist = event
    sends = []
    if kind == "P":
        if way is None:
            sends += [("P", 0, w, 1) for w in "RL" if reach(ring, "P", 0)[w] >= 1]
            first = 0
        else:
            if dist < reach(ring, "P", 0)[way]:
                sends.append(("P", 0, way, dist + 1))
            first = 2 * dist - 1 if way == "R" else 2 * dist
        sends += [("Q", first, w, 1) for w in "RL" if reach(ring, "Q", first)[w] >= 1]
    elif dist < reach(ring, "Q", k)[way]:
        sends.append(("Q", k, way, dist + 1))
    return sends


def event_order(ring, slab_us=0.7, hop_us=1.7, step_us=0.2):
    free = {"R": 0.0, "L": 0.0}
    arrivals, order, now, count = [], [], 0.0, 0
    pending = [("P", 0, None, 0)]
    while True:
        for event in pending:
            for sent in follow(ring, event):
                way = sent[2]
                free[way] = max(free[way], now) + slab_us
                count += 1
                heapq.heappush(arrivals, (free[way] + hop_us, count, sent))
        if not arrivals:
            return order
        when, _, event = heapq.heappop(arrivals)
        now = max(now + step_us, when)
        order.append(event)
        pending = [event]


def kernel(
    nx, ring, list_ref, hid_ref, tw_ref, dw_ref, loss_ref, gh_ref, gd_ref,
    wbuf, hb, acc, full, dall, msg, msgr, eown, lgall, crs, crsr, rss, rsr, rso, fsd, fin, ghs,
    init_sem, hid_sem, ag_send, ag_recv, xg_send, xg_recv, xr_send, lx_send, lx_recv, sm_send, sm_recv,
    lg_send, lg_recv, cr_send, cr_recv, rs_send, rs_recv, f_send, f_recv, gh_send, gh_recv, gh_loc,
):
    x = lax.axis_index("vocab")
    r = lax.axis_index("rows")
    c = lax.rem(r, 2)
    chip = r // 2
    y, z = chip // ring, lax.rem(chip, ring)
    p = y + c * (z - y)
    q = z + c * (y - z)
    half = ring // 2

    def mod(v):
        return lax.rem(v + 2 * ring, ring)

    def xmod(v):
        return lax.rem(v + nx, nx)

    def chip_of(pp, qq):
        straight, turned = pp * ring + qq, qq * ring + pp
        return straight + c * (turned - straight)

    def at(pp, qq):
        return (x, chip_of(mod(pp), mod(qq)) * 2 + c)

    partner = (x, chip * 2 + 1 - c)

    def rcopy(src, dst, ssem, rsem, dev):
        return pltpu.make_async_remote_copy(
            src_ref=src, dst_ref=dst, send_sem=ssem, recv_sem=rsem, device_id=dev, device_id_type=MESH
        )

    hid_local = pltpu.make_async_copy(hid_ref, hb.at[0:128], hid_sem.at[0])
    own = wbuf.at[p, q]
    loc_a0 = pltpu.make_async_copy(tw_ref.at[:, 0:256], own.at[0:64, :], init_sem.at[0])
    loc_b1 = pltpu.make_async_copy(tw_ref.at[:, 256:384], own.at[64:128, 0:128], init_sem.at[0])
    loc_b2 = pltpu.make_async_copy(dw_ref, own.at[64:128, 128:256], init_sem.at[1])

    @pl.when(c == 0)
    def _():
        loc_a0.start()

    @pl.when(c == 1)
    def _():
        loc_b1.start()
        loc_b2.start()

    hid_local.start()

    barrier = pltpu.get_barrier_semaphore()
    greeted = 0
    for d in range(1, ring):
        for core in (0, 1):
            for dev in ((mod(y + d) * ring + z), (y * ring + mod(z + d))):
                pl.semaphore_signal(barrier, inc=1, device_id=(x, dev * 2 + core), device_id_type=MESH)
                greeted += 1
    for d in range(1, nx):
        for core in (0, 1):
            pl.semaphore_signal(barrier, inc=1, device_id=(xmod(x + d), chip * 2 + core), device_id_type=MESH)
            greeted += 1
    pl.semaphore_signal(barrier, inc=1, device_id=partner, device_id_type=MESH)
    pl.semaphore_wait(barrier, greeted + 1)

    there = wbuf.at[q, p]
    to_b1 = rcopy(tw_ref.at[:, 256:384], there.at[0:64, 0:128], init_sem.at[2], init_sem.at[4], partner)
    to_b2 = rcopy(dw_ref, there.at[0:64, 128:256], init_sem.at[3], init_sem.at[5], partner)
    to_a = rcopy(tw_ref.at[:, 0:256], there.at[64:128, :], init_sem.at[2], init_sem.at[4], partner)
    from_a1 = rcopy(tw_ref.at[:, 256:384], own.at[0:64, 0:128], init_sem.at[2], init_sem.at[4], partner)
    from_a2 = rcopy(dw_ref, own.at[0:64, 128:256], init_sem.at[3], init_sem.at[5], partner)
    from_b = rcopy(tw_ref.at[:, 0:256], own.at[64:128, :], init_sem.at[2], init_sem.at[4], partner)

    @pl.when(c == 0)
    def _():
        to_b1.start()
        to_b2.start()

    @pl.when(c == 1)
    def _():
        to_a.start()

    hid_out = rcopy(hid_ref, hb.at[128:256], hid_sem.at[1], hid_sem.at[2], partner)
    hid_out.start()

    @pl.when(c == 0)
    def _():
        loc_a0.wait()
        from_b.wait_recv()

    @pl.when(c == 1)
    def _():
        loc_b1.wait()
        loc_b2.wait()
        from_a1.wait_recv()
        from_a2.wait_recv()

    events = event_order(ring)
    number = {event: i for i, event in enumerate(events)}

    def slab_pos(event):
        kind, k, way, dist = event
        step = -dist if way == "R" else dist
        if kind == "P":
            return mod(p + step), q
        return mod(p + offset_of(k)), mod(q + step)

    def send_along(sent, pos):
        kind, _, way, _ = sent
        step = 1 if way == "R" else -1
        dev = at(p + step, q) if kind == "P" else at(p, q + step)
        i = number[sent]
        slab = wbuf.at[pos[0], pos[1]]
        rcopy(slab, slab, ag_send.at[i], ag_recv.at[i], dev).start()

    def multiply(pos):
        pp, qq = pos
        lanes = pl.ds(pl.multiple_of(chip_of(pp, qq) * 128, 128), 128)
        acc[...] += jnp.dot(hb[:, lanes], wbuf[pp, qq], preferred_element_type=F32)

    def class_of(event):
        kind, k, way, dist = event
        if kind == "P":
            return (0, 0)
        if dist == half:
            return (1, half - 1)
        return (0, dist) if way == "L" else (1, dist - 1)

    left_in_class = {}
    for event in events:
        left_in_class[class_of(event)] = left_in_class.get(class_of(event), 0) + 1

    def class_q(h, i):
        return mod(q + i) if h == 0 else mod(q - 1 - i)

    def x_copies(h, i):
        src = wbuf.at[:, class_q(h, i), :, 128:256]
        dst = dall.at[x, i]
        out = []
        if nx > 1:
            out.append(rcopy(src, dst, xg_send.at[h, i, 0], xg_recv.at[0, i], (xmod(x + 1), chip * 2 + h)))
            out.append(rcopy(src, dst, xg_send.at[h, i, 1], xg_recv.at[1, i], (xmod(x - 1), chip * 2 + h)))
        if h == 0:
            out.append(rcopy(src, dst, xg_send.at[h, i, 2], xg_recv.at[3, i], (x, chip * 2)))
        else:
            out.append(pltpu.make_async_copy(src, dst, xg_recv.at[3, i]))
        return out

    def x_start(h, i):
        @pl.when(c == 1)
        def _():
            for copy in x_copies(h, i):
                copy.start()

    def x_arrived(kind, i):
        group = {0: xmod(x - 1), 1: xmod(x + 1), 2: xmod(x + 2), 3: x}[kind]
        slot = dall.at[group, i]
        return rcopy(slot, slot, xr_send.at[i], xg_recv.at[kind, i], (xmod(x + 1), r))

    def x_relay(i):
        if nx == 4:
            kind = i % 2
            x_arrived(kind, i).wait_recv()
            group = xmod(x - 1) if kind == 0 else xmod(x + 1)
            dev = (xmod(x + 1), r) if kind == 0 else (xmod(x - 1), r)
            slot = dall.at[group, i]
            rcopy(slot, slot, xr_send.at[i], xg_recv.at[2, i], dev).start()

    for sent in follow(ring, ("P", 0, None, 0)):
        send_along(sent, (p, q))
    acc[...] = jnp.zeros_like(acc)

    todo = [(p, q)]
    have_hidden = False
    held = []
    ready = []
    relayed = 0
    for n, event in enumerate(events):
        pos = slab_pos(event)
        slab = wbuf.at[pos[0], pos[1]]
        rcopy(slab, slab, ag_send.at[n], ag_recv.at[n], partner).wait_recv()
        for sent in follow(ring, event):
            send_along(sent, pos)
        cls = class_of(event)
        left_in_class[cls] -= 1
        if left_in_class[cls] == 0:
            if n < 0.7 * len(events):
                x_start(*cls)
                ready.append((cls[1], n))
            else:
                held.append(cls)
        if relayed < half and n >= 20:
            both = [m for i, m in ready if i == relayed]
            if len(both) == 2 and n >= max(both) + 12:
                x_relay(relayed)
                relayed += 1
        todo.append(pos)
        if n >= min(10, len(events) - 1):
            if not have_hidden:
                hid_local.wait()
                hid_out.wait_recv()
                have_hidden = True
            for _ in range(min(2, len(todo))):
                multiply(todo.pop(0))
    for pos in todo:
        multiply(pos)

    cols = pl.ds(pl.multiple_of(c * 256, 256), 256)
    lx = rcopy(acc.at[128:256], full.at[:, cols], lx_send, lx_recv, partner)
    lx.start()
    full[:, cols] = acc[0:128, :]
    other = full.at[:, pl.ds(pl.multiple_of((1 - c) * 256, 256), 256)]
    rcopy(other, other, lx_send, lx_recv, partner).wait_recv()

    t_logits = full[:, 0:384]
    d_logits = full[:, 384:512]
    t_max = jnp.max(t_logits, axis=1, keepdims=True)
    t_exp = jnp.exp(t_logits - t_max)
    t_sum = jnp.sum(t_exp, axis=1, keepdims=True)
    d_max = jnp.max(d_logits, axis=1, keepdims=True)
    d_sum = jnp.sum(jnp.exp(d_logits - d_max), axis=1, keepdims=True)
    covers = []
    for t in range(4):
        rows = slice(32 * t, 32 * t + 32)
        total = jnp.zeros((32, 128), F32)
        for d in range(nx):
            wanted = list_ref[t, xmod(x + d)]
            piece = jnp.zeros((32, 128), F32)
            for b in range(3):
                keep = jnp.where(wanted == 3 * x + b, 1.0, 0.0).astype(F32)
                piece += keep * t_exp[rows, 128 * b:128 * b + 128]
            if d == 0:
                eown[rows, :] = piece
            else:
                msg[d - 1, rows, :] = piece
            total += piece
        covers.append(jnp.sum(total, axis=1, keepdims=True))
    cover = jnp.concatenate(covers, axis=0)
    lane = lax.broadcasted_iota(jnp.int32, (128, 128), 1)
    stats = jnp.zeros((128, 128), F32)
    for i, value in enumerate((t_max, t_sum, cover, d_max, d_sum)):
        stats = jnp.where(lane == i, value, stats)
    stats_row = stats.T[0:8, :]
    for d in range(1, nx):
        msg[d - 1, 128:136, :] = stats_row

    def sm_copy(d):
        return rcopy(msg.at[d - 1], msgr.at[d - 1], sm_send.at[d - 1], sm_recv.at[d - 1], (xmod(x + d), r))

    for d in range(1, nx):
        sm_copy(d).start()
    for cls in held:
        x_start(*cls)
    for d in range(1, nx):
        sm_copy(d).wait_recv()
    stat = [(t_max, t_sum, cover, d_max, d_sum)]
    for d in range(1, nx):
        got = jnp.concatenate([msgr[d - 1, 128:136, :]] * 16, axis=0).T
        stat.append(tuple(got[:, i:i + 1] for i in range(5)))
    all_tmax = functools.reduce(jnp.maximum, [s[0] for s in stat])
    all_dmax = functools.reduce(jnp.maximum, [s[3] for s in stat])
    t_scale = [jnp.exp(s[0] - all_tmax) for s in stat]
    all_tsum = sum(s[1] * a for s, a in zip(stat, t_scale))
    all_dsum = sum(s[4] * jnp.exp(s[3] - all_dmax) for s in stat)
    covered = sum(s[2] * a for s, a in zip(stat, t_scale)) / all_tsum
    target = eown[...] * (t_scale[0] / all_tsum)
    for d in range(1, nx):
        target += msgr[d - 1, 0:128, :] * (t_scale[d] / all_tsum)
    prob = jnp.exp(d_logits - all_dmax) / all_dsum
    lgall[x, 0:128, :] = (covered * prob - target).astype(BF16)

    def lg_copies():
        src = lgall.at[x, 0:128]
        out = [rcopy(src, lgall.at[x, 128:256], lg_send.at[0, 1], lg_recv.at[0, 1], partner)]
        for d in range(1, nx):
            xx = xmod(x + d)
            out.append(rcopy(src, lgall.at[x, 0:128], lg_send.at[d, 0], lg_recv.at[d, 0], (xx, r)))
            out.append(
                rcopy(src, lgall.at[x, 128:256], lg_send.at[d, 1], lg_recv.at[d, 1], (xx, chip * 2 + 1 - c))
            )
        return out

    def lg_wait(d, side):
        group = xmod(x - d)
        slot = lgall.at[group, 128 * side:128 * side + 128]
        rcopy(slot, slot, lg_send.at[d, side], lg_recv.at[d, side], partner).wait_recv()

    for copy in lg_copies():
        copy.start()
    crossed = jnp.sum(target * d_logits, axis=1, keepdims=True)
    crs[...] = jnp.broadcast_to(crossed, (128, 128)).T[0:8, :]

    def cr_copy(d):
        return rcopy(crs, crsr.at[d - 1], cr_send.at[d - 1], cr_recv.at[d - 1], (xmod(x + d), r))

    for d in range(1, nx):
        cr_copy(d).start()

    lg_wait(0, 1)
    lg_t = lgall[x].astype(F32).T.astype(BF16)
    odd = lax.rem(p + q + c, 2)

    def partial(pp, i):
        qq = 2 * i + lax.rem(pp + c, 2)
        lanes = pl.ds(pl.multiple_of(chip_of(pp, qq) * 128, 128), 128)
        return jnp.dot(lg_t, hb[:, lanes], preferred_element_type=F32)

    def rs_copy(d):
        return rcopy(rss.at[d - 1], rsr.at[d - 1], rs_send.at[d - 1], rs_recv.at[d - 1], at(p + d, q))

    for d in sorted(range(1, ring), key=lambda d: -min(d, ring - d)):
        for i in range(half):
            rss[d - 1, i] = partial(mod(p + d), i).astype(BF16)
        rs_copy(d).start()
    for i in range(half):
        rso[i] = partial(p, i)

    for i in range(relayed, half):
        x_relay(i)
    loss = covered * (all_dmax + jnp.log(all_dsum))
    loss_row = jnp.broadcast_to(loss, (128, 128)).T[0:8, :] - crs[...]
    for d in range(1, nx):
        cr_copy(d).wait_recv()
        loss_row -= crsr[d - 1]
    loss_ref[...] = loss_row

    for d in range(1, nx):
        for side in (0, 1):
            lg_wait(d, side)

    wide = ring * 128

    def gh_copies(i):
        qq = mod(q + i) if False else None
        yy = mod(y + i - c * (1 + 2 * i))
        lanes = pl.ds(pl.multiple_of(yy * wide, wide), wide)
        mine = pltpu.make_async_copy(ghs.at[i, 0:128], gh_ref.at[:, lanes], gh_loc.at[i])
        theirs = rcopy(ghs.at[i, 128:256], gh_ref.at[:, lanes], gh_send.at[i], gh_recv.at[i], partner)
        return mine, theirs

    for i in range(half):
        if nx > 1:
            for kind in (0, 1, 2):
                if kind == i % 2 or (kind == 2 and nx != 4):
                    continue
                x_arrived(kind, i).wait_recv()

        @pl.when(c == 0)
        def _():
            x_arrived(3, i).wait_recv()

        @pl.when(c == 1)
        def _():
            pltpu.make_async_copy(wbuf.at[:, class_q(1, i), :, 128:256], dall.at[x, i], xg_recv.at[3, i]).wait()

        def width(s, carry):
            summed = jnp.zeros((256, 128), F32)
            for g in range(nx):
                piece = lax.dot_general(lgall[g], dall[g, i, s], NT, preferred_element_type=F32)
                summed += piece.astype(BF16).astype(F32)
            ghs[i, :, pl.ds(pl.multiple_of(s * 128, 128), 128)] = summed.astype(BF16)
            return carry

        lax.fori_loop(0, ring, width, 0)
        for copy in gh_copies(i):
            copy.start()

    for d in range(1, ring):
        rs_copy(d).wait_recv()

    def add_up(i, carry):
        total = rso[i]
        for d in range(1, ring):
            total += rsr[d - 1, i].astype(F32)
        fsd[i] = total.T
        return carry

    lax.fori_loop(0, half, add_up, 0)

    def f_copy(i, core):
        d = odd + 2 * i
        qq = mod(q + d)
        j = (qq - lax.rem(p + c, 2)) // 2
        dev = (x, chip_of(p, qq) * 2 + core)
        return rcopy(
            fsd.at[j, 64 * core:64 * core + 64], fin.at[d], f_send.at[i, core], f_recv.at[d], dev
        )

    def f_stays(i, core):
        return jnp.logical_and(odd + 2 * i == 0, core == c)

    for i in range(half):
        for core in (0, 1):
            stays = f_stays(i, core)

            @pl.when(jnp.logical_not(stays))
            def _():
                f_copy(i, core).start()

            @pl.when(stays)
            def _():
                j = (q - lax.rem(p + c, 2)) // 2
                fin[0] = fsd[j, 64 * core:64 * core + 64, :]

    home = lax.rem(y + z + c, 2) == 0
    grad = jnp.zeros((64, 128), F32)
    for d in range(ring):
        slot = fin.at[d]
        arrival = rcopy(slot, slot, f_send.at[0, 0], f_recv.at[d], partner)
        if d == 0:
            pl.when(jnp.logical_not(home))(arrival.wait_recv)
        else:
            arrival.wait_recv()
        grad += fin[d]
    gd_ref[...] = grad

    for i in range(half):
        mine, theirs = gh_copies(i)
        mine.wait()
        theirs.wait_send()
    for i in range(half):
        mine, theirs = gh_copies(i)
        theirs.wait_recv()
    for i in range(half):
        for core in (0, 1):
            @pl.when(jnp.logical_not(f_stays(i, core)))
            def _():
                f_copy(i, core).wait_send()
    for d in range(1, ring):
        rs_copy(d).wait_send()
    for d in range(1, nx):
        cr_copy(d).wait_send()
        sm_copy(d).wait_send()
    for copy in lg_copies():
        copy.wait_send()
    lx.wait_send()
    hid_out.wait_send()

    @pl.when(c == 0)
    def _():
        to_b1.wait_send()
        to_b2.wait_send()

    @pl.when(c == 1)
    def _():
        to_a.wait_send()
        for h in (0, 1):
            for i in range(half):
                for n, copy in enumerate(x_copies(h, i)):
                    if nx > 1 and n < 2 or h == 0:
                        copy.wait_send()

    if nx == 4:
        for i in range(half):
            x_arrived(0, i).wait_send()
    for n, event in enumerate(events):
        slab = wbuf.at[0, 0]
        rcopy(slab, slab, ag_send.at[n], ag_recv.at[n], partner).wait_send()


def per_device(nx, ring, hidden, teacher_weight, draft_weight, draft_list):
    tiles, tile_rows, width = hidden.shape
    rows = tiles * tile_rows
    half = ring // 2
    dma = pltpu.SemaphoreType.DMA
    more = max(nx - 1, 1)
    scratch = [
        pltpu.VMEM((ring, ring, 128, 256), BF16),
        pltpu.VMEM((2 * rows, width), BF16),
        pltpu.VMEM((2 * rows, 256), F32),
        pltpu.VMEM((rows, 512), F32),
        pltpu.VMEM((nx, half, ring, 128, 128), BF16),
        pltpu.VMEM((more, rows + 8, 128), F32),
        pltpu.VMEM((more, rows + 8, 128), F32),
        pltpu.VMEM((rows, 128), F32),
        pltpu.VMEM((nx, 2 * rows, 128), BF16),
        pltpu.VMEM((8, 128), F32),
        pltpu.VMEM((more, 8, 128), F32),
        pltpu.VMEM((ring - 1, half, 128, 128), BF16),
        pltpu.VMEM((ring - 1, half, 128, 128), BF16),
        pltpu.VMEM((half, 128, 128), F32),
        pltpu.VMEM((half, 128, 128), F32),
        pltpu.VMEM((ring, 64, 128), F32),
        pltpu.VMEM((half, 2 * rows, ring * 128), BF16),
        dma((6,)), dma((3,)), dma((ring * ring,)), dma((ring * ring,)),
        dma((2, half, 3)), dma((4, half)), dma((half,)),
        dma(()), dma(()), dma((more,)), dma((more,)),
        dma((nx, 2)), dma((nx, 2)), dma((more,)), dma((more,)),
        dma((ring - 1,)), dma((ring - 1,)), dma((half, 2)), dma((ring,)),
        dma((half,)), dma((half,)), dma((half,)),
    ]
    hbm = pl.BlockSpec(memory_space=pl.ANY)
    vmem = pl.BlockSpec(memory_space=pltpu.VMEM)
    loss, grad_hidden, grad_draft = pl.pallas_call(
        functools.partial(kernel, nx, ring),
        out_shape=(
            jax.ShapeDtypeStruct((8, 128), F32),
            jax.ShapeDtypeStruct((rows, width), BF16),
            jax.ShapeDtypeStruct((64, 128), F32),
        ),
        in_specs=[pl.BlockSpec(memory_space=pltpu.SMEM), hbm, hbm, hbm],
        out_specs=(vmem, hbm, vmem),
        scratch_shapes=scratch,
        compiler_params=pltpu.CompilerParams(
            collective_id=0, has_side_effects=True, vmem_limit_bytes=48 * 1024 * 1024
        ),
        name="distill",
    )(draft_list, hidden.reshape(rows, width), teacher_weight, draft_weight)
    return loss[0].reshape(tiles, tile_rows), grad_hidden.reshape(hidden.shape), grad_draft


def solution(mesh):
    nx, devices = mesh.shape["vocab"], mesh.shape["rows"]
    ring = int(round((devices // 2) ** 0.5))
    in_specs = (P(None, "rows", None), P("rows", "vocab"), P("rows", "vocab"), P())
    out_specs = (P(None, "rows"), P(None, "rows", None), P("rows", "vocab"))
    return jax.shard_map(
        functools.partial(per_device, nx, ring), mesh=mesh, in_specs=in_specs, out_specs=out_specs, check_vma=False
    )
```

time: 502 us -> 100 us (0.20)
  waiting for transfers between devices: 428 us -> 0 us
  Pallas kernels: 0 us -> 93.1 us
  blocking collectives: 27.8 us -> 0 us
  between operations: 13.8 us -> 0.65 us
  matrix products: 12.8 us -> 0 us
  local copies, waits for them, and re-layouts: 13.1 us -> 6.4 us
    unnamed x5 -> x0, waiting for transfers between devices: 204 us -> none
    all_gather x2 -> x0, waiting for transfers between devices: 165 us -> none  [the longest x1 89.8 us: per_device(): draft_full = lax.all_gather(draft_weight, 'rows', axis=0, tiled=True)]
    pallas_call x0 -> x1, Pallas kernels: none -> 93.1 us  [per_device(): pl.pallas_call(functools.partial(kernel, nx, ring), out_shape=(jax.ShapeD...]
    psum x1 -> x0, waiting for transfers between devices: 59.9 us -> none  [per_device(): lax.psum(partial_value.astype(jnp.bfloat16), 'vocab')]
    dot_general x4 -> x0, matrix products: 12.8 us -> none  [the longest x1 4.05 us: per_device(): jnp.dot(columns, lax.all_gather(teacher_weight, 'rows', axis=0, tiled=Tru...]
    all_gather x1 -> x0, blocking collectives: 11.9 us -> none  [per_device(): teacher_all = lax.all_gather(teacher_logits, 'vocab', axis=1, tiled=True)]
    pmax x1 -> x0, blocking collectives: 8.41 us -> none  [per_device(): draft_max = lax.pmax(local_max, 'vocab')]
    psum x1 -> x0, blocking collectives: 7.51 us -> none  [per_device(): draft_total, crossed = lax.psum((local_total, weighted), 'vocab')]
  transfers between devices with their start and end apart: 4 -> 0, of which waited for: 4 -> 0; matrix products, arithmetic and copies ran while one was open for 3% -> 0% of each run, Pallas kernels for 0% -> 0%
where the time goes in v1:
time: 100 us
  Pallas kernels  93.1 us (93%)
  local copies, waits for them, and re-layouts  6.4 us (6%)
    pallas_call x1, Pallas kernels, per_device(): pl.pallas_call(functools.partial(kernel, nx, ring), out_shape=(jax.ShapeD...  93.1 us
    unnamed x10, local copies, waits for them, and re-layouts  5.71 us

profile of v1, /device:TPU:1, one launch (start us, length us, event | category | flops | bytes accessed | tf_op | source)
XLA Modules:
  0.0 100.1 jit_solution(4557185097678871085)
XLA Ops:
  0.6 0.0 copy-start
  0.6 1.6 %copy-done = bf16[4,32,8192]{2,1,0:T(8,128)(2,1)S(1)} copy-done((bf16[4,32,8192]{2,1,0:T(8,128)(2,1)S(1)}, bf16[4,32,8192]{2,1,0:T(8,128)(2,1)}, u32[]{:S(2)}) %copy-start) | copy-done | bytes 2097176
  2.2 0.0 copy-start.1
  2.2 0.8 copy-done.1
  3.0 0.0 copy-start.2
  3.0 0.7 copy-done.2
  3.7 0.0 copy-start.3
  3.7 0.7 copy-done.3
  4.4 93.1 %distill.1 = (f32[8,128]{1,0:T(8,128)S(1)}, bf16[128,8192]{1,0:T(8,128)(2,1)S(1)}, f32[64,128]{1,0:T(8,128)S(1)}) custom-call(s32[4,4]{1,0:T(4,128)S(1)} %copy-done.3, bf16[128,8192]{1,0:T(8,128)(2,1)S(1)} %bitcast.2, bf16[64,384]{1,0:T(8,128)(2,1)S(1)} %copy-done.1, bf16[64,128]{1,0:T(8,128)(2,1)S(1)} %copy-done.2), custom_call_target="tpu_custom_call" | custom-call | tf_op jit(solution)/shard_map/distill/pallas_call | solution.py:559
  97.5 0.7 reshape_squeeze.3
  98.2 1.3 %copy.9 = bf16[4,32,8192]{2,1,0:T(8,128)(2,1)} copy(bf16[4,32,8192]{2,1,0:T(8,128)(2,1)S(1)} %bitcast.3) | data formatting | bytes 4194304
  99.5 0.6 copy.10
  (1 shorter events, 0.0 us)
Async XLA Ops:
  0.6 1.6 %copy-start = (bf16[4,32,8192]{2,1,0:T(8,128)(2,1)S(1)}, bf16[4,32,8192]{2,1,0:T(8,128)(2,1)}, u32[]{:S(2)}) copy-start(bf16[4,32,8192]{2,1,0:T(8,128)(2,1)} %param.4) | copy-start | bytes 6291460
  2.2 0.8 copy-start.1
  3.0 0.7 copy-start.2
  3.7 0.7 copy-start.3

commit v2 on v1

--- a/solution.py
+++ b/solution.py
@@ -8,7 +8,7 @@
 from jax.experimental.pallas import tpu as pltpu
 from jax.sharding import PartitionSpec as P
 
-BLK = 128
+CHUNKS = 8
 F32 = jnp.float32
 BF16 = jnp.bfloat16
 MESH = pl.DeviceIdType.MESH
@@ -64,9 +64,10 @@
 
 def kernel(
     nx, ring, list_ref, hid_ref, tw_ref, dw_ref, loss_ref, gh_ref, gd_ref,
-    wbuf, hb, acc, full, dall, msg, msgr, eown, lgall, crs, crsr, rss, rsr, rso, fsd, fin, ghs,
-    init_sem, hid_sem, ag_send, ag_recv, xg_send, xg_recv, xr_send, lx_send, lx_recv, sm_send, sm_recv,
+    wbuf, hb, acc, full, dall, dq, msg, msgr, eown, lgall, crs, crsr, rss, rsr, rso, fsd, fin, ghs,
+    init_sem, hid_sem, ag_send, ag_recv, xg_send, xg_recv, xr_send, dq_send, dq_recv, lx_send, lx_recv, sm_send, sm_recv,
     lg_send, lg_recv, cr_send, cr_recv, rs_send, rs_recv, f_send, f_recv, gh_send, gh_recv, gh_loc,
+    gx_send, gx_recv, gy_send,
 ):
     x = lax.axis_index("vocab")
     r = lax.axis_index("rows")
@@ -76,6 +77,8 @@
     p = y + c * (z - y)
     q = z + c * (y - z)
     half = ring // 2
+    whole = half // 2
+    part = ring // nx
 
     def mod(v):
         return lax.rem(v + 2 * ring, ring)
@@ -211,10 +214,23 @@
             out.append(pltpu.make_async_copy(src, dst, xg_recv.at[3, i]))
         return out
 
+    def dq_copies(h, i):
+        out = []
+        for d in range(nx):
+            xx = xmod(x + d)
+            src = wbuf.at[pl.ds(part * xx, part), class_q(h, i), :, 128:256]
+            dst = dq.at[x, i - whole]
+            if d == 0 and h == 1:
+                out.append(pltpu.make_async_copy(src, dst, dq_recv.at[0, i - whole]))
+            else:
+                dev = (xx, chip * 2 + h)
+                out.append(rcopy(src, dst, dq_send.at[h, i - whole, d], dq_recv.at[d, i - whole], dev))
+        return out
+
     def x_start(h, i):
         @pl.when(c == 1)
         def _():
-            for copy in x_copies(h, i):
+            for copy in x_copies(h, i) if i < whole else dq_copies(h, i):
                 copy.start()
 
     def x_arrived(kind, i):
@@ -249,14 +265,14 @@
         cls = class_of(event)
         left_in_class[cls] -= 1
         if left_in_class[cls] == 0:
-            if n < 0.7 * len(events):
+            if cls[1] < whole:
                 x_start(*cls)
                 ready.append((cls[1], n))
             else:
                 held.append(cls)
-        if relayed < half and n >= 20:
+        if relayed < whole - 1:
             both = [m for i, m in ready if i == relayed]
-            if len(both) == 2 and n >= max(both) + 12:
+            if len(both) == 2 and n >= max(both) + 18:
                 x_relay(relayed)
                 relayed += 1
         todo.append(pos)
@@ -316,6 +332,8 @@
         sm_copy(d).start()
     for cls in held:
         x_start(*cls)
+    for i in range(relayed, whole):
+        x_relay(i)
     for d in range(1, nx):
         sm_copy(d).wait_recv()
     stat = [(t_max, t_sum, cover, d_max, d_sum)]
@@ -380,8 +398,6 @@
     for i in range(half):
         rso[i] = partial(p, i)
 
-    for i in range(relayed, half):
-        x_relay(i)
     loss = covered * (all_dmax + jnp.log(all_dsum))
     loss_row = jnp.broadcast_to(loss, (128, 128)).T[0:8, :] - crs[...]
     for d in range(1, nx):
@@ -394,19 +410,81 @@
             lg_wait(d, side)
 
     wide = ring * 128
+    piece_wide = part * 128
+
+    def class_y(h, i):
+        return mod(y + i - h * (1 + 2 * i))
+
+    def gh_lanes(h, i, xx):
+        if i < whole:
+            return pl.ds(pl.multiple_of(class_y(h, i) * wide, wide), wide)
+        return pl.ds(pl.multiple_of(class_y(h, i) * wide + xx * piece_wide, piece_wide), piece_wide)
+
+    def gh_src(i, side):
+        return ghs.at[i, 128 * side:128 * side + 128, 0:wide if i < whole else piece_wide]
 
     def gh_copies(i):
-        qq = mod(q + i) if False else None
-        yy = mod(y + i - c * (1 + 2 * i))
-        lanes = pl.ds(pl.multiple_of(yy * wide, wide), wide)
-        mine = pltpu.make_async_copy(ghs.at[i, 0:128], gh_ref.at[:, lanes], gh_loc.at[i])
-        theirs = rcopy(ghs.at[i, 128:256], gh_ref.at[:, lanes], gh_send.at[i], gh_recv.at[i], partner)
+        lanes = gh_lanes(c, i, x)
+        mine = pltpu.make_async_copy(gh_src(i, 0), gh_ref.at[:, lanes], gh_loc.at[i])
+        theirs = rcopy(gh_src(i, 1), gh_ref.at[:, lanes], gh_send.at[i], gh_recv.at[i], partner)
         return mine, theirs
 
-    for i in range(half):
+    def gx_copies(i):
+        out = []
+        if nx > 1:
+            lanes = gh_lanes(c, i, x)
+            for side in (0, 1):
+                core = chip * 2 + (c if side == 0 else 1 - c)
+                for kind, xx in ((0, xmod(x + 1)), (1, xmod(x - 1))):
+                    out.append(
+                        rcopy(
+                            gh_src(i, side), gh_ref.at[:, lanes], gx_send.at[side, i - whole, kind],
+                            gx_recv.at[side, i - whole, kind], (xx, core),
+                        )
+                    )
+        return out
+
+    def gx_arrived(side, i, kind):
+        h = c if side == 0 else 1 - c
+        xx = {0: xmod(x - 1), 1: xmod(x + 1), 2: xmod(x + 2)}[kind]
+        slot = gh_ref.at[:, gh_lanes(h, i, xx)]
+        return rcopy(slot, slot, gy_send.at[side, i - whole], gx_recv.at[side, i - whole, kind], (xmod(x + 1), r))
+
+    def gx_relay(side, i):
+        kind = (i - whole) % 2
+        gx_arrived(side, i, kind).wait_recv()
+        h = c if side == 0 else 1 - c
+        slot = gh_ref.at[:, gh_lanes(h, i, xmod(x - 1) if kind == 0 else xmod(x + 1))]
+        dev = (xmod(x + 1) if kind == 0 else xmod(x - 1), r)
+        rcopy(slot, slot, gy_send.at[side, i - whole], gx_recv.at[side, i - whole, 2], dev).start()
+
+    for i in range(whole, half):
+        for d in range(nx):
+            slot = dq.at[xmod(x - d), i - whole]
+            if d == 0:
+                @pl.when(c == 1)
+                def _():
+                    dq_copies(1, i)[0].wait()
+
+                @pl.when(c == 0)
+                def _():
+                    rcopy(slot, slot, dq_send.at[0, 0, 0], dq_recv.at[0, i - whole], partner).wait_recv()
+            else:
+                rcopy(slot, slot, dq_send.at[0, 0, 0], dq_recv.at[d, i - whole], partner).wait_recv()
+
+        for s in range(part):
+            summed = jnp.zeros((256, 128), F32)
+            for g in range(nx):
+                piece = lax.dot_general(lgall[g], dq[g, i - whole, s], NT, preferred_element_type=F32)
+                summed += piece.astype(BF16).astype(F32)
+            ghs[i, :, 128 * s:128 * s + 128] = summed.astype(BF16)
+        for copy in (*gx_copies(i), *gh_copies(i)):
+            copy.start()
+
+    for i in range(whole):
         if nx > 1:
             for kind in (0, 1, 2):
-                if kind == i % 2 or (kind == 2 and nx != 4):
+                if kind == i % 2:
                     continue
                 x_arrived(kind, i).wait_recv()
 
@@ -429,6 +507,11 @@
         lax.fori_loop(0, ring, width, 0)
         for copy in gh_copies(i):
             copy.start()
+
+    if nx == 4:
+        for i in range(whole, half):
+            for side in (0, 1):
+                gx_relay(side, i)
 
     for d in range(1, ring):
         rs_copy(d).wait_recv()
@@ -484,8 +567,17 @@
         mine.wait()
         theirs.wait_send()
     for i in range(half):
-        mine, theirs = gh_copies(i)
-        theirs.wait_recv()
+        slot = gh_ref.at[:, gh_lanes(1 - c, i, x)]
+        rcopy(slot, slot, gh_send.at[i], gh_recv.at[i], partner).wait_recv()
+    if nx == 4:
+        for i in range(whole, half):
+            for side in (0, 1):
+                for kind in (0, 1, 2):
+                    if kind != (i - whole) % 2:
+                        gx_arrived(side, i, kind).wait_recv()
+                gx_arrived(side, i, 0).wait_send()
+            for copy in gx_copies(i):
+                copy.wait_send()
     for i in range(half):
         for core in (0, 1):
             @pl.when(jnp.logical_not(f_stays(i, core)))
@@ -510,23 +602,54 @@
     def _():
         to_a.wait_send()
         for h in (0, 1):
-            for i in range(half):
+            for i in range(whole):
                 for n, copy in enumerate(x_copies(h, i)):
                     if nx > 1 and n < 2 or h == 0:
                         copy.wait_send()
+            for i in range(whole, half):
+                for d, copy in enumerate(dq_copies(h, i)):
+                    if d > 0 or h == 0:
+                        copy.wait_send()
 
     if nx == 4:
-        for i in range(half):
+        for i in range(whole):
             x_arrived(0, i).wait_send()
     for n, event in enumerate(events):
         slab = wbuf.at[0, 0]
         rcopy(slab, slab, ag_send.at[n], ag_recv.at[n], partner).wait_send()
 
 
+def deliver(tiles, loss_in, gh_in, gd_in, loss_out, gh_out, gd_out, wide_loss, loss_buf, gh_buf, gd_buf, come, go):
+    rows = gh_in.shape[0] // CHUNKS
+    chunks = [slice(rows * n, rows * n + rows) for n in range(CHUNKS)]
+    take_loss = pltpu.make_async_copy(loss_in, wide_loss, come.at[CHUNKS])
+    take_gd = pltpu.make_async_copy(gd_in, gd_buf, come.at[CHUNKS + 1])
+    put_loss = pltpu.make_async_copy(loss_buf, loss_out, go.at[CHUNKS])
+    put_gd = pltpu.make_async_copy(gd_buf, gd_out, go.at[CHUNKS + 1])
+    take = [pltpu.make_async_copy(gh_in.at[k], gh_buf.at[k], come.at[n]) for n, k in enumerate(chunks)]
+    put = [pltpu.make_async_copy(gh_buf.at[k], gh_out.at[k], go.at[n]) for n, k in enumerate(chunks)]
+    for copy in (take_loss, take_gd, *take):
+        copy.start()
+    take_loss.wait()
+    lanes = loss_buf.shape[1]
+    for t in range(tiles):
+        loss_buf[t:t + 1, :] = wide_loss[0:1, lanes * t:lanes * t + lanes]
+    put_loss.start()
+    take_gd.wait()
+    put_gd.start()
+    for taken, given in zip(take, put):
+        taken.wait()
+        given.start()
+    for copy in (put_loss, put_gd, *put):
+        copy.wait()
+
+
 def per_device(nx, ring, hidden, teacher_weight, draft_weight, draft_list):
     tiles, tile_rows, width = hidden.shape
     rows = tiles * tile_rows
     half = ring // 2
+    whole = half // 2
+    parts = half - whole
     dma = pltpu.SemaphoreType.DMA
     more = max(nx - 1, 1)
     scratch = [
@@ -534,7 +657,8 @@
         pltpu.VMEM((2 * rows, width), BF16),
         pltpu.VMEM((2 * rows, 256), F32),
         pltpu.VMEM((rows, 512), F32),
-        pltpu.VMEM((nx, half, ring, 128, 128), BF16),
+        pltpu.VMEM((nx, max(whole, 1), ring, 128, 128), BF16),
+        pltpu.VMEM((nx, half - whole, ring // nx, 128, 128), BF16),
         pltpu.VMEM((more, rows + 8, 128), F32),
         pltpu.VMEM((more, rows + 8, 128), F32),
         pltpu.VMEM((rows, 128), F32),
@@ -548,11 +672,12 @@
         pltpu.VMEM((ring, 64, 128), F32),
         pltpu.VMEM((half, 2 * rows, ring * 128), BF16),
         dma((6,)), dma((3,)), dma((ring * ring,)), dma((ring * ring,)),
-        dma((2, half, 3)), dma((4, half)), dma((half,)),
+        dma((2, half, 3)), dma((4, half)), dma((half,)), dma((2, parts, nx)), dma((nx, parts)),
         dma(()), dma(()), dma((more,)), dma((more,)),
         dma((nx, 2)), dma((nx, 2)), dma((more,)), dma((more,)),
         dma((ring - 1,)), dma((ring - 1,)), dma((half, 2)), dma((ring,)),
         dma((half,)), dma((half,)), dma((half,)),
+        dma((2, parts, 2)), dma((2, parts, 3)), dma((2, parts)),
     ]
     hbm = pl.BlockSpec(memory_space=pl.ANY)
     vmem = pl.BlockSpec(memory_space=pltpu.VMEM)
@@ -567,11 +692,27 @@
         out_specs=(vmem, hbm, vmem),
         scratch_shapes=scratch,
         compiler_params=pltpu.CompilerParams(
-            collective_id=0, has_side_effects=True, vmem_limit_bytes=48 * 1024 * 1024
+            collective_id=0, has_side_effects=True, vmem_limit_bytes=60 * 1024 * 1024
         ),
         name="distill",
     )(draft_list, hidden.reshape(rows, width), teacher_weight, draft_weight)
-    return loss[0].reshape(tiles, tile_rows), grad_hidden.reshape(hidden.shape), grad_draft
+    loss, grad_hidden, grad_draft = pl.pallas_call(
+        functools.partial(deliver, tiles),
+        out_shape=(
+            jax.ShapeDtypeStruct((tiles, tile_rows), F32),
+            jax.ShapeDtypeStruct((rows, width), BF16),
+            jax.ShapeDtypeStruct((64, 128), F32),
+        ),
+        in_specs=[hbm, hbm, hbm],
+        out_specs=(hbm, hbm, hbm),
+        scratch_shapes=[
+            pltpu.VMEM((8, 128), F32), pltpu.VMEM((tiles, tile_rows), F32), pltpu.VMEM((rows, width), BF16),
+            pltpu.VMEM((64, 128), F32), dma((CHUNKS + 2,)), dma((CHUNKS + 2,)),
+        ],
+        compiler_params=pltpu.CompilerParams(vmem_limit_bytes=60 * 1024 * 1024),
+        name="deliver",
+    )(loss, grad_hidden, grad_draft)
+    return loss, grad_hidden.reshape(hidden.shape), grad_draft
 
 
 def solution(mesh):

time: 100 us -> 90.8 us (0.908)
  local copies, waits for them, and re-layouts: 6.4 us -> 0 us
  Pallas kernels: 93.1 us -> 89.9 us
    unnamed x10 -> x0, local copies, waits for them, and re-layouts: 5.71 us -> none
    pallas_call x1, Pallas kernels: 93.1 us -> 87.5 us  [per_device(): pl.pallas_call(functools.partial(kernel, nx, ring), out_shape=(jax.ShapeD...]
    pallas_call x0 -> x1, Pallas kernels: none -> 2.45 us  [per_device(): pl.pallas_call(functools.partial(deliver, tiles), out_shape=(jax.ShapeDty...]
where the time goes in v2:
time: 90.8 us; the launch traced here: 90.6 us
  Pallas kernels  89.9 us (99%)
    pallas_call x1, Pallas kernels, per_device(): pl.pallas_call(functools.partial(kernel, nx, ring), out_shape=(jax.ShapeD...  87.5 us
    pallas_call x1, Pallas kernels, per_device(): pl.pallas_call(functools.partial(deliver, tiles), out_shape=(jax.ShapeDty...  2.45 us

profile of v2, /device:TPU:1, one launch (start us, length us, event | category | flops | bytes accessed | tf_op | source)
XLA Modules:
  0.0 90.6 jit_solution(4441988142790849532)
XLA Ops:
  0.6 87.5 %distill.1 = (f32[8,128]{1,0:T(8,128)}, bf16[128,8192]{1,0:T(8,128)(2,1)}, f32[64,128]{1,0:T(8,128)}) custom-call(s32[4,4]{1,0:T(4,128)} %list_ref.1, bf16[128,8192]{1,0:T(8,128)(2,1)} %bitcast.2, bf16[64,384]{1,0:T(8,128)(2,1)} %tw_ref.1, bf16[64,128]{1,0:T(8,128)(2,1)} %dw_ref.1), custom_call_target="tpu_custom_call" | custom-call | tf_op jit(solution)/shard_map/distill/pallas_call | solution.py:684
  88.1 2.5 %deliver.1 = (f32[4,32]{1,0:T(4,128)}, bf16[128,8192]{1,0:T(8,128)(2,1)}, f32[64,128]{1,0:T(8,128)}) custom-call(f32[8,128]{1,0:T(8,128)} %get-tuple-element.9.loss_in, bf16[128,8192]{1,0:T(8,128)(2,1)} %get-tuple-element.10.gh_in, f32[64,128]{1,0:T(8,128)} %get-tuple-element.11.gd_in), custom_call_target="tpu_custom_call" | custom-call | tf_op jit(solution)/shard_map/deliver/pallas_call | solution.py:699

commit v3 on v2

--- a/solution.py
+++ b/solution.py
@@ -64,8 +64,8 @@
 
 def kernel(
     nx, ring, list_ref, hid_ref, tw_ref, dw_ref, loss_ref, gh_ref, gd_ref,
-    wbuf, hb, acc, full, dall, dq, msg, msgr, eown, lgall, crs, crsr, rss, rsr, rso, fsd, fin, ghs,
-    init_sem, hid_sem, ag_send, ag_recv, xg_send, xg_recv, xr_send, dq_send, dq_recv, lx_send, lx_recv, sm_send, sm_recv,
+    wbuf, hb, acc, full, dall, dq, msg, msgr, stm, stmr, eown, lgall, crs, crsr, rss, rsr, rso, fsd, fin, ghs,
+    init_sem, hid_sem, ag_send, ag_recv, xg_send, xg_recv, xr_send, dq_send, dq_recv, lx_send, lx_recv, sm_send, sm_recv, st_send, st_recv,
     lg_send, lg_recv, cr_send, cr_recv, rs_send, rs_recv, f_send, f_recv, gh_send, gh_recv, gh_loc,
     gx_send, gx_recv, gy_send,
 ):
@@ -254,8 +254,7 @@
     todo = [(p, q)]
     have_hidden = False
     held = []
-    ready = []
-    relayed = 0
+    relay_at = {}
     for n, event in enumerate(events):
         pos = slab_pos(event)
         slab = wbuf.at[pos[0], pos[1]]
@@ -267,14 +266,11 @@
         if left_in_class[cls] == 0:
             if cls[1] < whole:
                 x_start(*cls)
-                ready.append((cls[1], n))
+                relay_at.setdefault(n + 16, []).append(cls)
             else:
                 held.append(cls)
-        if relayed < whole - 1:
-            both = [m for i, m in ready if i == relayed]
-            if len(both) == 2 and n >= max(both) + 18:
-                x_relay(relayed)
-                relayed += 1
+        for h, i in relay_at.pop(n, ()):
+            pl.when(c == h)(functools.partial(x_relay, i))
         todo.append(pos)
         if n >= min(10, len(events) - 1):
             if not have_hidden:
@@ -298,13 +294,17 @@
     t_max = jnp.max(t_logits, axis=1, keepdims=True)
     t_exp = jnp.exp(t_logits - t_max)
     t_sum = jnp.sum(t_exp, axis=1, keepdims=True)
-    d_max = jnp.max(d_logits, axis=1, keepdims=True)
-    d_sum = jnp.sum(jnp.exp(d_logits - d_max), axis=1, keepdims=True)
-    covers = []
-    for t in range(4):
-        rows = slice(32 * t, 32 * t + 32)
-        total = jnp.zeros((32, 128), F32)
-        for d in range(nx):
+
+    def sm_copy(d):
+        return rcopy(msg.at[d - 1], msgr.at[d - 1], sm_send.at[d - 1], sm_recv.at[d - 1], (xmod(x + d), r))
+
+    def st_copy(d):
+        return rcopy(stm, stmr.at[d - 1], st_send.at[d - 1], st_recv.at[d - 1], (xmod(x + d), r))
+
+    totals = [jnp.zeros((32, 128), F32) for _ in range(4)]
+    for d in sorted(range(nx), key=lambda d: -min(d, nx - d)):
+        for t in range(4):
+            rows = slice(32 * t, 32 * t + 32)
             wanted = list_ref[t, xmod(x + d)]
             piece = jnp.zeros((32, 128), F32)
             for b in range(3):
@@ -313,32 +313,30 @@
             if d == 0:
                 eown[rows, :] = piece
             else:
-                msg[d - 1, rows, :] = piece
-            total += piece
-        covers.append(jnp.sum(total, axis=1, keepdims=True))
-    cover = jnp.concatenate(covers, axis=0)
+                msg[d - 1, rows, :] = piece.astype(BF16)
+            totals[t] += piece
+        if d > 0:
+            sm_copy(d).start()
+    cover = jnp.concatenate([jnp.sum(total, axis=1, keepdims=True) for total in totals], axis=0)
+    d_max = jnp.max(d_logits, axis=1, keepdims=True)
+    d_sum = jnp.sum(jnp.exp(d_logits - d_max), axis=1, keepdims=True)
     lane = lax.broadcasted_iota(jnp.int32, (128, 128), 1)
     stats = jnp.zeros((128, 128), F32)
     for i, value in enumerate((t_max, t_sum, cover, d_max, d_sum)):
         stats = jnp.where(lane == i, value, stats)
-    stats_row = stats.T[0:8, :]
-    for d in range(1, nx):
-        msg[d - 1, 128:136, :] = stats_row
-
-    def sm_copy(d):
-        return rcopy(msg.at[d - 1], msgr.at[d - 1], sm_send.at[d - 1], sm_recv.at[d - 1], (xmod(x + d), r))
-
-    for d in range(1, nx):
-        sm_copy(d).start()
+    stm[...] = stats.T[0:8, :]
+    for d in range(1, nx):
+        st_copy(d).start()
     for cls in held:
         x_start(*cls)
-    for i in range(relayed, whole):
-        x_relay(i)
-    for d in range(1, nx):
-        sm_copy(d).wait_recv()
+    for n in sorted(relay_at):
+        for h, i in relay_at[n]:
+            pl.when(c == h)(functools.partial(x_relay, i))
+    for d in range(1, nx):
+        st_copy(d).wait_recv()
     stat = [(t_max, t_sum, cover, d_max, d_sum)]
     for d in range(1, nx):
-        got = jnp.concatenate([msgr[d - 1, 128:136, :]] * 16, axis=0).T
+        got = jnp.concatenate([stmr[d - 1]] * 16, axis=0).T
         stat.append(tuple(got[:, i:i + 1] for i in range(5)))
     all_tmax = functools.reduce(jnp.maximum, [s[0] for s in stat])
     all_dmax = functools.reduce(jnp.maximum, [s[3] for s in stat])
@@ -347,9 +345,10 @@
     all_dsum = sum(s[4] * jnp.exp(s[3] - all_dmax) for s in stat)
     covered = sum(s[2] * a for s, a in zip(stat, t_scale)) / all_tsum
     target = eown[...] * (t_scale[0] / all_tsum)
-    for d in range(1, nx):
-        target += msgr[d - 1, 0:128, :] * (t_scale[d] / all_tsum)
     prob = jnp.exp(d_logits - all_dmax) / all_dsum
+    for d in range(1, nx):
+        sm_copy(d).wait_recv()
+        target += msgr[d - 1].astype(F32) * (t_scale[d] / all_tsum)
     lgall[x, 0:128, :] = (covered * prob - target).astype(BF16)
 
     def lg_copies():
@@ -520,7 +519,7 @@
         total = rso[i]
         for d in range(1, ring):
             total += rsr[d - 1, i].astype(F32)
-        fsd[i] = total.T
+        fsd[i] = total.T.astype(BF16)
         return carry
 
     lax.fori_loop(0, half, add_up, 0)
@@ -559,7 +558,7 @@
             pl.when(jnp.logical_not(home))(arrival.wait_recv)
         else:
             arrival.wait_recv()
-        grad += fin[d]
+        grad += fin[d].astype(F32)
     gd_ref[...] = grad
 
     for i in range(half):
@@ -588,6 +587,7 @@
     for d in range(1, nx):
         cr_copy(d).wait_send()
         sm_copy(d).wait_send()
+        st_copy(d).wait_send()
     for copy in lg_copies():
         copy.wait_send()
     lx.wait_send()
@@ -659,8 +659,10 @@
         pltpu.VMEM((rows, 512), F32),
         pltpu.VMEM((nx, max(whole, 1), ring, 128, 128), BF16),
         pltpu.VMEM((nx, half - whole, ring // nx, 128, 128), BF16),
-        pltpu.VMEM((more, rows + 8, 128), F32),
-        pltpu.VMEM((more, rows + 8, 128), F32),
+        pltpu.VMEM((more, rows, 128), BF16),
+        pltpu.VMEM((more, rows, 128), BF16),
+        pltpu.VMEM((8, 128), F32),
+        pltpu.VMEM((more, 8, 128), F32),
         pltpu.VMEM((rows, 128), F32),
         pltpu.VMEM((nx, 2 * rows, 128), BF16),
         pltpu.VMEM((8, 128), F32),
@@ -668,12 +670,12 @@
         pltpu.VMEM((ring - 1, half, 128, 128), BF16),
         pltpu.VMEM((ring - 1, half, 128, 128), BF16),
         pltpu.VMEM((half, 128, 128), F32),
-        pltpu.VMEM((half, 128, 128), F32),
-        pltpu.VMEM((ring, 64, 128), F32),
+        pltpu.VMEM((half, 128, 128), BF16),
+        pltpu.VMEM((ring, 64, 128), BF16),
         pltpu.VMEM((half, 2 * rows, ring * 128), BF16),
         dma((6,)), dma((3,)), dma((ring * ring,)), dma((ring * ring,)),
         dma((2, half, 3)), dma((4, half)), dma((half,)), dma((2, parts, nx)), dma((nx, parts)),
-        dma(()), dma(()), dma((more,)), dma((more,)),
+        dma(()), dma(()), dma((more,)), dma((more,)), dma((more,)), dma((more,)),
         dma((nx, 2)), dma((nx, 2)), dma((more,)), dma((more,)),
         dma((ring - 1,)), dma((ring - 1,)), dma((half, 2)), dma((ring,)),
         dma((half,)), dma((half,)), dma((half,)),

time: 90.8 us -> 85.2 us (0.938)
  Pallas kernels: 89.9 us -> 84.4 us
    pallas_call x1, Pallas kernels: 87.5 us -> 81.9 us  [per_device(): pl.pallas_call(functools.partial(kernel, nx, ring), out_shape=(jax.ShapeD...]
where the time goes in v3:
time: 85.2 us; the launch traced here: 85 us
  Pallas kernels  84.4 us (99%)
    pallas_call x1, Pallas kernels, per_device(): pl.pallas_call(functools.partial(kernel, nx, ring), out_shape=(jax.ShapeD...  81.9 us
    pallas_call x1, Pallas kernels, per_device(): pl.pallas_call(functools.partial(deliver, tiles), out_shape=(jax.ShapeDty...  2.45 us

profile of v3, /device:TPU:1, one launch (start us, length us, event | category | flops | bytes accessed | tf_op | source)
XLA Modules:
  0.0 85.0 jit_solution(12169018346850630301)
XLA Ops:
  0.6 81.9 %distill.1 = (f32[8,128]{1,0:T(8,128)}, bf16[128,8192]{1,0:T(8,128)(2,1)}, f32[64,128]{1,0:T(8,128)}) custom-call(s32[4,4]{1,0:T(4,128)} %list_ref.1, bf16[128,8192]{1,0:T(8,128)(2,1)} %bitcast.2, bf16[64,384]{1,0:T(8,128)(2,1)} %tw_ref.1, bf16[64,128]{1,0:T(8,128)(2,1)} %dw_ref.1), custom_call_target="tpu_custom_call" | custom-call | tf_op jit(solution)/shard_map/distill/pallas_call | solution.py:686
  82.6 2.5 %deliver.1 = (f32[4,32]{1,0:T(4,128)}, bf16[128,8192]{1,0:T(8,128)(2,1)}, f32[64,128]{1,0:T(8,128)}) custom-call(f32[8,128]{1,0:T(8,128)} %get-tuple-element.9.loss_in, bf16[128,8192]{1,0:T(8,128)(2,1)} %get-tuple-element.10.gh_in, f32[64,128]{1,0:T(8,128)} %get-tuple-element.11.gd_in), custom_call_target="tpu_custom_call" | custom-call | tf_op jit(solution)/shard_map/deliver/pallas_call | solution.py:701

commit v4 on v3

--- a/solution.py
+++ b/solution.py
@@ -101,7 +101,7 @@
         )
 
     hid_local = pltpu.make_async_copy(hid_ref, hb.at[0:128], hid_sem.at[0])
-    own = wbuf.at[p, q]
+    own = wbuf.at[y, z]
     loc_a0 = pltpu.make_async_copy(tw_ref.at[:, 0:256], own.at[0:64, :], init_sem.at[0])
     loc_b1 = pltpu.make_async_copy(tw_ref.at[:, 256:384], own.at[64:128, 0:128], init_sem.at[0])
     loc_b2 = pltpu.make_async_copy(dw_ref, own.at[64:128, 128:256], init_sem.at[1])
@@ -131,10 +131,9 @@
     pl.semaphore_signal(barrier, inc=1, device_id=partner, device_id_type=MESH)
     pl.semaphore_wait(barrier, greeted + 1)
 
-    there = wbuf.at[q, p]
-    to_b1 = rcopy(tw_ref.at[:, 256:384], there.at[0:64, 0:128], init_sem.at[2], init_sem.at[4], partner)
-    to_b2 = rcopy(dw_ref, there.at[0:64, 128:256], init_sem.at[3], init_sem.at[5], partner)
-    to_a = rcopy(tw_ref.at[:, 0:256], there.at[64:128, :], init_sem.at[2], init_sem.at[4], partner)
+    to_b1 = rcopy(tw_ref.at[:, 256:384], own.at[0:64, 0:128], init_sem.at[2], init_sem.at[4], partner)
+    to_b2 = rcopy(dw_ref, own.at[0:64, 128:256], init_sem.at[3], init_sem.at[5], partner)
+    to_a = rcopy(tw_ref.at[:, 0:256], own.at[64:128, :], init_sem.at[2], init_sem.at[4], partner)
     from_a1 = rcopy(tw_ref.at[:, 256:384], own.at[0:64, 0:128], init_sem.at[2], init_sem.at[4], partner)
     from_a2 = rcopy(dw_ref, own.at[0:64, 128:256], init_sem.at[3], init_sem.at[5], partner)
     from_b = rcopy(tw_ref.at[:, 0:256], own.at[64:128, :], init_sem.at[2], init_sem.at[4], partner)
@@ -166,25 +165,31 @@
     events = event_order(ring)
     number = {event: i for i, event in enumerate(events)}
 
-    def slab_pos(event):
+    def slab_pos(net, event):
         kind, k, way, dist = event
         step = -dist if way == "R" else dist
-        if kind == "P":
-            return mod(p + step), q
-        return mod(p + offset_of(k)), mod(q + step)
-
-    def send_along(sent, pos):
+        first, second = (step, 0) if kind == "P" else (offset_of(k), step)
+        return (mod(y + first), mod(z + second)) if net == 0 else (mod(y + second), mod(z + first))
+
+    def half_slab(net, pos):
+        return wbuf.at[pos[0], pos[1], :, 128 * net:128 * net + 128]
+
+    def send_along(net, sent, pos):
         kind, _, way, _ = sent
         step = 1 if way == "R" else -1
-        dev = at(p + step, q) if kind == "P" else at(p, q + step)
+        if (kind == "P") == (net == 0):
+            dev = mod(y + step) * ring + z
+        else:
+            dev = y * ring + mod(z + step)
         i = number[sent]
-        slab = wbuf.at[pos[0], pos[1]]
-        rcopy(slab, slab, ag_send.at[i], ag_recv.at[i], dev).start()
-
-    def multiply(pos):
-        pp, qq = pos
-        lanes = pl.ds(pl.multiple_of(chip_of(pp, qq) * 128, 128), 128)
-        acc[...] += jnp.dot(hb[:, lanes], wbuf[pp, qq], preferred_element_type=F32)
+        slab = half_slab(net, pos)
+        rcopy(slab, slab, ag_send.at[net, i], ag_recv.at[net, i], (x, dev * 2 + c)).start()
+
+    def multiply(net, pos):
+        yy, zz = pos
+        lanes = pl.ds(pl.multiple_of((yy * ring + zz) * 128, 128), 128)
+        columns = slice(128 * net, 128 * net + 128)
+        acc[:, columns] += jnp.dot(hb[:, lanes], wbuf[yy, zz, :, columns], preferred_element_type=F32)
 
     def class_of(event):
         kind, k, way, dist = event
@@ -198,11 +203,11 @@
     for event in events:
         left_in_class[class_of(event)] = left_in_class.get(class_of(event), 0) + 1
 
-    def class_q(h, i):
-        return mod(q + i) if h == 0 else mod(q - 1 - i)
+    def class_y(h, i):
+        return mod(y + i - h * (1 + 2 * i))
 
     def x_copies(h, i):
-        src = wbuf.at[:, class_q(h, i), :, 128:256]
+        src = wbuf.at[class_y(h, i), :, :, 128:256]
         dst = dall.at[x, i]
         out = []
         if nx > 1:
@@ -218,7 +223,7 @@
         out = []
         for d in range(nx):
             xx = xmod(x + d)
-            src = wbuf.at[pl.ds(part * xx, part), class_q(h, i), :, 128:256]
+            src = wbuf.at[class_y(h, i), pl.ds(part * xx, part), :, 128:256]
             dst = dq.at[x, i - whole]
             if d == 0 and h == 1:
                 out.append(pltpu.make_async_copy(src, dst, dq_recv.at[0, i - whole]))
@@ -248,19 +253,22 @@
             rcopy(slot, slot, xr_send.at[i], xg_recv.at[2, i], dev).start()
 
     for sent in follow(ring, ("P", 0, None, 0)):
-        send_along(sent, (p, q))
+        for net in (0, 1):
+            send_along(net, sent, (y, z))
     acc[...] = jnp.zeros_like(acc)
 
-    todo = [(p, q)]
+    todo = [(0, (y, z)), (1, (y, z))]
     have_hidden = False
     held = []
     relay_at = {}
     for n, event in enumerate(events):
-        pos = slab_pos(event)
-        slab = wbuf.at[pos[0], pos[1]]
-        rcopy(slab, slab, ag_send.at[n], ag_recv.at[n], partner).wait_recv()
-        for sent in follow(ring, event):
-            send_along(sent, pos)
+        for net in (0, 1):
+            pos = slab_pos(net, event)
+            slab = half_slab(net, pos)
+            rcopy(slab, slab, ag_send.at[net, n], ag_recv.at[net, n], partner).wait_recv()
+            for sent in follow(ring, event):
+                send_along(net, sent, pos)
+            todo.append((net, pos))
         cls = class_of(event)
         left_in_class[cls] -= 1
         if left_in_class[cls] == 0:
@@ -271,16 +279,15 @@
                 held.append(cls)
         for h, i in relay_at.pop(n, ()):
             pl.when(c == h)(functools.partial(x_relay, i))
-        todo.append(pos)
         if n >= min(10, len(events) - 1):
             if not have_hidden:
                 hid_local.wait()
                 hid_out.wait_recv()
                 have_hidden = True
-            for _ in range(min(2, len(todo))):
-                multiply(todo.pop(0))
-    for pos in todo:
-        multiply(pos)
+            for _ in range(min(4, len(todo))):
+                multiply(*todo.pop(0))
+    for job in todo:
+        multiply(*job)
 
     cols = pl.ds(pl.multiple_of(c * 256, 256), 256)
     lx = rcopy(acc.at[128:256], full.at[:, cols], lx_send, lx_recv, partner)
@@ -411,9 +418,6 @@
     wide = ring * 128
     piece_wide = part * 128
 
-    def class_y(h, i):
-        return mod(y + i - h * (1 + 2 * i))
-
     def gh_lanes(h, i, xx):
         if i < whole:
             return pl.ds(pl.multiple_of(class_y(h, i) * wide, wide), wide)
@@ -493,7 +497,7 @@
 
         @pl.when(c == 1)
         def _():
-            pltpu.make_async_copy(wbuf.at[:, class_q(1, i), :, 128:256], dall.at[x, i], xg_recv.at[3, i]).wait()
+            pltpu.make_async_copy(wbuf.at[class_y(1, i), :, :, 128:256], dall.at[x, i], xg_recv.at[3, i]).wait()
 
         def width(s, carry):
             summed = jnp.zeros((256, 128), F32)
@@ -506,11 +510,6 @@
         lax.fori_loop(0, ring, width, 0)
         for copy in gh_copies(i):
             copy.start()
-
-    if nx == 4:
-        for i in range(whole, half):
-            for side in (0, 1):
-                gx_relay(side, i)
 
     for d in range(1, ring):
         rs_copy(d).wait_recv()
@@ -548,6 +547,11 @@
             def _():
                 j = (q - lax.rem(p + c, 2)) // 2
                 fin[0] = fsd[j, 64 * core:64 * core + 64, :]
+
+    if nx == 4:
+        for i in range(whole, half):
+            for side in (0, 1):
+                gx_relay(side, i)
 
     home = lax.rem(y + z + c, 2) == 0
     grad = jnp.zeros((64, 128), F32)
@@ -615,8 +619,9 @@
         for i in range(whole):
             x_arrived(0, i).wait_send()
     for n, event in enumerate(events):
-        slab = wbuf.at[0, 0]
-        rcopy(slab, slab, ag_send.at[n], ag_recv.at[n], partner).wait_send()
+        for net in (0, 1):
+            slab = half_slab(net, (0, 0))
+            rcopy(slab, slab, ag_send.at[net, n], ag_recv.at[net, n], partner).wait_send()
 
 
 def deliver(tiles, loss_in, gh_in, gd_in, loss_out, gh_out, gd_out, wide_loss, loss_buf, gh_buf, gd_buf, come, go):
@@ -673,7 +678,7 @@
         pltpu.VMEM((half, 128, 128), BF16),
         pltpu.VMEM((ring, 64, 128), BF16),
         pltpu.VMEM((half, 2 * rows, ring * 128), BF16),
-        dma((6,)), dma((3,)), dma((ring * ring,)), dma((ring * ring,)),
+        dma((6,)), dma((3,)), dma((2, ring * ring)), dma((2, ring * ring)),
         dma((2, half, 3)), dma((4, half)), dma((half,)), dma((2, parts, nx)), dma((nx, parts)),
         dma(()), dma(()), dma((more,)), dma((more,)), dma((more,)), dma((more,)),
         dma((nx, 2)), dma((nx, 2)), dma((more,)), dma((more,)),

time: 85.2 us -> 82.7 us (0.971)
  Pallas kernels: 84.4 us -> 81.9 us
    pallas_call x1, Pallas kernels: 81.9 us -> 79.5 us  [per_device(): pl.pallas_call(functools.partial(kernel, nx, ring), out_shape=(jax.ShapeD...]
where the time goes in v4:
time: 82.7 us; the launch traced here: 82.6 us
  Pallas kernels  81.9 us (99%)
    pallas_call x1, Pallas kernels, per_device(): pl.pallas_call(functools.partial(kernel, nx, ring), out_shape=(jax.ShapeD...  79.5 us
    pallas_call x1, Pallas kernels, per_device(): pl.pallas_call(functools.partial(deliver, tiles), out_shape=(jax.ShapeDty...  2.45 us

profile of v4, /device:TPU:1, one launch (start us, length us, event | category | flops | bytes accessed | tf_op | source)
XLA Modules:
  0.0 82.6 jit_solution(1495022526592745072)
XLA Ops:
  0.6 79.5 %distill.1 = (f32[8,128]{1,0:T(8,128)}, bf16[128,8192]{1,0:T(8,128)(2,1)}, f32[64,128]{1,0:T(8,128)}) custom-call(s32[4,4]{1,0:T(4,128)} %list_ref.1, bf16[128,8192]{1,0:T(8,128)(2,1)} %bitcast.2, bf16[64,384]{1,0:T(8,128)(2,1)} %tw_ref.1, bf16[64,128]{1,0:T(8,128)(2,1)} %dw_ref.1), custom_call_target="tpu_custom_call" | custom-call | tf_op jit(solution)/shard_map/distill/pallas_call | solution.py:691
  80.1 2.5 %deliver.1 = (f32[4,32]{1,0:T(4,128)}, bf16[128,8192]{1,0:T(8,128)(2,1)}, f32[64,128]{1,0:T(8,128)}) custom-call(f32[8,128]{1,0:T(8,128)} %get-tuple-element.9.loss_in, bf16[128,8192]{1,0:T(8,128)(2,1)} %get-tuple-element.10.gh_in, f32[64,128]{1,0:T(8,128)} %get-tuple-element.11.gd_in), custom_call_target="tpu_custom_call" | custom-call | tf_op jit(solution)/shard_map/deliver/pallas_call | solution.py:706

commit v5 on v4

--- a/solution.py
+++ b/solution.py
@@ -185,11 +185,13 @@
         slab = half_slab(net, pos)
         rcopy(slab, slab, ag_send.at[net, i], ag_recv.at[net, i], (x, dev * 2 + c)).start()
 
-    def multiply(net, pos):
-        yy, zz = pos
-        lanes = pl.ds(pl.multiple_of((yy * ring + zz) * 128, 128), 128)
+    def multiply(net, jobs):
         columns = slice(128 * net, 128 * net + 128)
-        acc[:, columns] += jnp.dot(hb[:, lanes], wbuf[yy, zz, :, columns], preferred_element_type=F32)
+        total = acc[:, columns]
+        for yy, zz in jobs:
+            lanes = pl.ds(pl.multiple_of((yy * ring + zz) * 128, 128), 128)
+            total += jnp.dot(hb[:, lanes], wbuf[yy, zz, :, columns], preferred_element_type=F32)
+        acc[:, columns] = total
 
     def class_of(event):
         kind, k, way, dist = event
@@ -257,7 +259,7 @@
             send_along(net, sent, (y, z))
     acc[...] = jnp.zeros_like(acc)
 
-    todo = [(0, (y, z)), (1, (y, z))]
+    todo = [[(y, z)], [(y, z)]]
     have_hidden = False
     held = []
     relay_at = {}
@@ -268,7 +270,7 @@
             rcopy(slab, slab, ag_send.at[net, n], ag_recv.at[net, n], partner).wait_recv()
             for sent in follow(ring, event):
                 send_along(net, sent, pos)
-            todo.append((net, pos))
+            todo[net].append(pos)
         cls = class_of(event)
         left_in_class[cls] -= 1
         if left_in_class[cls] == 0:
@@ -284,10 +286,13 @@
                 hid_local.wait()
                 hid_out.wait_recv()
                 have_hidden = True
-            for _ in range(min(4, len(todo))):
-                multiply(*todo.pop(0))
-    for job in todo:
-        multiply(*job)
+            jobs = todo[n % 2][:4]
+            del todo[n % 2][:4]
+            if jobs:
+                multiply(n % 2, jobs)
+    for net in (0, 1):
+        if todo[net]:
+            multiply(net, todo[net])
 
     cols = pl.ds(pl.multiple_of(c * 256, 256), 256)
     lx = rcopy(acc.at[128:256], full.at[:, cols], lx_send, lx_recv, partner)

time: 82.7 us -> 82.6 us (level)
  no operation moved by 1% of the time
where the time goes in v5:
time: 82.6 us; the launch traced here: 82.4 us
  Pallas kernels  81.8 us (99%)
    pallas_call x1, Pallas kernels, per_device(): pl.pallas_call(functools.partial(kernel, nx, ring), out_shape=(jax.ShapeD...  79.3 us
    pallas_call x1, Pallas kernels, per_device(): pl.pallas_call(functools.partial(deliver, tiles), out_shape=(jax.ShapeDty...  2.45 us

profile of v5, /device:TPU:1, one launch (start us, length us, event | category | flops | bytes accessed | tf_op | source)
XLA Modules:
  0.0 82.4 jit_solution(18006080306743069550)
XLA Ops:
  0.6 79.3 %distill.1 = (f32[8,128]{1,0:T(8,128)}, bf16[128,8192]{1,0:T(8,128)(2,1)}, f32[64,128]{1,0:T(8,128)}) custom-call(s32[4,4]{1,0:T(4,128)} %list_ref.1, bf16[128,8192]{1,0:T(8,128)(2,1)} %bitcast.2, bf16[64,384]{1,0:T(8,128)(2,1)} %tw_ref.1, bf16[64,128]{1,0:T(8,128)(2,1)} %dw_ref.1), custom_call_target="tpu_custom_call" | custom-call | tf_op jit(solution)/shard_map/distill/pallas_call | solution.py:696
  80.0 2.5 %deliver.1 = (f32[4,32]{1,0:T(4,128)}, bf16[128,8192]{1,0:T(8,128)(2,1)}, f32[64,128]{1,0:T(8,128)}) custom-call(f32[8,128]{1,0:T(8,128)} %get-tuple-element.9.loss_in, bf16[128,8192]{1,0:T(8,128)(2,1)} %get-tuple-element.10.gh_in, f32[64,128]{1,0:T(8,128)} %get-tuple-element.11.gd_in), custom_call_target="tpu_custom_call" | custom-call | tf_op jit(solution)/shard_map/deliver/pallas_call | solution.py:711
